TPU v7x, 32 devices: a whole 2x2x4 slice. The times are simulated.
32 devices in a mesh: dp: 8 (over z, y), seq: 4 (over x, core).
Axes of the slice: x: 2, y: 2, z: 4, core: 2. Of those that a mesh axis runs over, the one named last changes fastest.
Arguments:
- tokens: bfloat16 [8, 512, 1024], P('dp', 'seq'), may hold values from -6 to 6
- cache_keys: bfloat16 [8, 2048, 1024], P('dp', 'seq')
- cache_values: bfloat16 [8, 2048, 1024], P('dp', 'seq'), may hold values from -6 to 6
- qkv_weight: bfloat16 [1024, 3072], P(None, 'seq'), may hold values from -0.1875 to 0.1875
- qkv_bias: float32 [3072], replicated, may hold values from -3 to 3
- out_weight: bfloat16 [1024, 1024], P('seq', 'dp'), may hold values from -0.1875 to 0.1875
- out_bias: float32 [1024], replicated, may hold values from -3 to 3
- norm_gain: float32 [1024], replicated, may hold values from 0.1 to 1.9
- norm_bias: float32 [1024], replicated, may hold values from -3 to 3
- cached_len: int32 [8], replicated, may hold values from 0 to 2048, as said below
- span_len: int32 [8], replicated, may hold values from 1 to 512, as said below
- slot_request: int32 [8], replicated, may hold values from 0 to 7, each once
Outputs:
- normed: bfloat16 [8, 512, 1024], P('dp', 'seq')
Inputs may be any that keep to these rules, and one draw needn't show every extreme that they name: `cached_len`: some request has exactly 2048 cached positions. `span_len`: some request has exactly 512 new tokens in use. `slot_request`: each request names one slot.
All inputs are finite; a program needn't handle non-finite values.
Results may differ from a plain program's by a relative error of at most 0.0085.
Values may be sent and summed in bfloat16 or wider, within the bound.
A program may use at most 64 MiB of HBM per device.

v0:
```python
import jax
import jax.numpy as jnp
from jax import lax
from jax.sharding import PartitionSpec as P

D = 1024
HEADS = 16
HEAD_DIM = 64
neg_big = -1e30


def local(
    tokens,
    cache_keys,
    cache_values,
    qkv_weight,
    qkv_bias,
    out_weight,
    out_bias,
    norm_gain,
    norm_bias,
    cached_len,
    span_len,
    slot_request,
):
    seq_index = lax.axis_index("seq")
    dp_index = lax.axis_index("dp")
    groups = lax.axis_size("seq")
    request = slot_request[dp_index]
    cached = cached_len[request]
    filled = span_len[request]
    inputs = tokens[0]
    own_rows = inputs.shape[0]
    cache_rows = cache_keys.shape[1]
    all_rows = own_rows * groups
    scale = HEAD_DIM ** (-0.5)
    qkv_full = lax.all_gather(qkv_weight, "seq", axis=1, tiled=True)
    summed = jnp.dot(inputs, qkv_full, preferred_element_type=jnp.float32)
    projected = (summed + qkv_bias).astype(jnp.bfloat16)
    split = projected.reshape(own_rows, HEADS, 3, HEAD_DIM)
    own_queries = split[:, :, 0].reshape(own_rows, D)
    new_keys = split[:, :, 1].reshape(own_rows, D)
    new_values = split[:, :, 2].reshape(own_rows, D)
    all_queries = lax.all_gather(own_queries, "seq", axis=0, tiled=True)
    keys = jnp.concatenate([cache_keys[0], new_keys], 0)
    values = jnp.concatenate([cache_values[0], new_values], 0)
    positions = jnp.arange(all_rows)
    cache_pos = seq_index * cache_rows + jnp.arange(cache_rows)
    new_pos = seq_index * own_rows + jnp.arange(own_rows)
    live_cache = jnp.broadcast_to(cache_pos[None, :] < cached, (all_rows, cache_rows))
    live_new = (new_pos[None, :] <= positions[:, None]) & (new_pos[None, :] < filled)
    live = jnp.concatenate([live_cache, live_new], 1)

    def attend(head, carry):
        outputs, tops, totals = carry
        start = head * HEAD_DIM
        query = lax.dynamic_slice_in_dim(all_queries, start, HEAD_DIM, 1)
        key_block = lax.dynamic_slice_in_dim(keys, start, HEAD_DIM, 1)
        value_block = lax.dynamic_slice_in_dim(values, start, HEAD_DIM, 1)
        scores = (
            lax.dot_general(
                query, key_block, (((1,), (1,)), ((), ())), preferred_element_type=jnp.float32
            )
            * scale
        )
        masked = jnp.where(live, scores, neg_big)
        top = jnp.max(masked, axis=1)
        weights = jnp.where(live, jnp.exp(masked - top[:, None]), 0.0)
        total = jnp.sum(weights, axis=1)
        numer = jnp.dot(
            weights.astype(jnp.bfloat16), value_block, preferred_element_type=jnp.float32
        )
        result = (numer / jnp.maximum(total, 1.0)[:, None]).astype(jnp.bfloat16)
        outputs = lax.dynamic_update_slice_in_dim(outputs, result, start, 1)
        tops = lax.dynamic_update_slice(tops, top[:, None], (0, head))
        totals = lax.dynamic_update_slice(totals, total[:, None], (0, head))
        return (outputs, tops, totals)

    start_state = (
        jnp.zeros((all_rows, D), jnp.bfloat16),
        jnp.zeros((all_rows, HEADS), jnp.float32),
        jnp.zeros((all_rows, HEADS), jnp.float32),
    )
    partial_value, tops, totals = lax.fori_loop(0, HEADS, attend, start_state)
    partial_wide = partial_value.astype(jnp.float32)
    every_partial, every_top, every_total = (
        lax.all_gather(partial_wide[None], "seq", axis=0, tiled=True),
        lax.all_gather(tops[None], "seq", axis=0, tiled=True),
        lax.all_gather(totals[None], "seq", axis=0, tiled=True),
    )
    mine_partial = lax.dynamic_slice_in_dim(every_partial, seq_index * own_rows, own_rows, 1)
    mine_top = lax.dynamic_slice_in_dim(every_top, seq_index * own_rows, own_rows, 1)
    mine_total = lax.dynamic_slice_in_dim(every_total, seq_index * own_rows, own_rows, 1)
    best = jnp.max(mine_top, axis=0)
    share = mine_total * jnp.exp(mine_top - best[None])
    denom = jnp.sum(share, axis=0)
    spread_parts = mine_partial.reshape(groups, own_rows, HEADS, HEAD_DIM)
    attn = (
        (jnp.sum(share[:, :, :, None] * spread_parts, axis=0) / denom[:, :, None])
        .reshape(own_rows, D)
        .astype(jnp.bfloat16)
    )
    head_rows = lax.all_gather(out_weight, "dp", axis=1, tiled=True)
    out_full = lax.all_gather(head_rows, "seq", axis=0, tiled=True)
    projected_out = jnp.dot(attn, out_full, preferred_element_type=jnp.float32)
    mixed = projected_out + out_bias + inputs.astype(jnp.float32)
    center = mixed - jnp.mean(mixed, axis=1, keepdims=True)
    variance = jnp.mean(center * center, axis=1, keepdims=True)
    normed = (center * lax.rsqrt(variance + 1e-05) * norm_gain + norm_bias).astype(jnp.bfloat16)
    return normed[None]


def solution(mesh):
    return jax.shard_map(
        local,
        mesh=mesh,
        in_specs=(
            P("dp", "seq", None),
            P("dp", "seq", None),
            P("dp", "seq", None),
            P(None, "seq"),
            P(),
            P("seq", "dp"),
            P(),
            P(),
            P(),
            P(),
            P(),
            P(),
        ),
        out_specs=P("dp", "seq", None),
        check_vma=False,
    )
```

profile of v0, /device:TPU:0, one launch (start us, length us, event | category | flops | bytes accessed | tf_op | source)
XLA Modules:
  0.0 230.9 jit_solution(1036459860229054314)
XLA Ops:
  7.3 50.7 %all-gather.8.cloned.1.call-done = bf16[1024,3072]{1,0:T(8,128)(2,1)} async-done(((bf16[1024,768]{1,0:T(8,128)(2,1)}), bf16[1024,3072]{1,0:T(8,128)(2,1)}) %all-gather.8.cloned.1.call-update) | async-done | bytes 6291472 | tf_op jit(solution)/shard_map/all_gather | solution.py:37
  58.0 3.8 %fusion.15 = bf16[128,3072]{1,0:T(8,128)(2,1)S(1)} fusion(bf16[1024,3072]{1,0:T(8,128)(2,1)} %all-gather.8.cloned.1.call-done, f32[3072]{0:T(1024)S(1)} %copy-done.3, bf16[1,128,1024]{2,1,0:T(8,128)(2,1)S(1)} %copy-done), kind=kOutput, calls=%fused_computation.19 | convolution fusion | flops 806092800 | bytes 7352320 | tf_op jit(solution)/shard_map/dot_general | solution.py:38
  68.4 2.6 %pad_maximum_fusion = (bf16[640,1024]{1,0:T(8,128)(2,1)S(1)}, bf16[640,1024]{1,0:T(8,128)(2,1)}) fusion(bf16[128,1024]{1,0:T(8,128)(2,1)S(1)} %copy.14, bf16[512,1024]{1,0:T(8,128)(2,1)S(1)} %bitcast.39, bf16[128,1024]{1,0:T(8,128)(2,1)S(1)} %copy.15, bf16[512,1024]{1,0:T(8,128)(2,1)} %bitcast.40), kind=kLoop, calls=%fused_computation.22 | loop fusion | flops 5242880 | bytes 5242880 | tf_op jit(solution)/shard_map/concatenate | solution.py:45
  71.0 9.1 %all-gather.10.cloned.1.call-done = bf16[512,1024]{0,1:T(8,128)(2,1)} async-done(((bf16[128,1024]{0,1:T(8,128)(2,1)}), bf16[512,1024]{0,1:T(8,128)(2,1)}) %all-gather.10.cloned.1.call-update) | async-done | bytes 1048592 | tf_op jit(solution)/shard_map/all_gather | solution.py:44
  80.1 55.4 %while.17 = (s32[]{:T(128)}, bf16[512,1024]{0,1:T(8,128)(2,1)S(1)}, f32[512,16]{0,1:T(8,128)S(1)}, f32[512,16]{0,1:T(8,128)S(1)}, bf16[512,1024]{0,1:T(8,128)(2,...) while((s32[]{:T(128)}, bf16[512,1024]{0,1:T(8,128)(2,1)S(1)}, ...), condition=%wide.region_3.4_spmd, body=%wide.region_0.3_spmd.sunk | while | flops 86900224 | bytes 5398699 | solution.py:84
  82.0 1.4 fusion.43
  85.5 1.4 fusion.43
  92.4 1.4 fusion.43
  99.3 1.4 fusion.43
  109.7 1.4 fusion.43
  113.2 1.4 fusion.43
  116.7 1.4 fusion.43
  123.6 1.4 fusion.43
  130.5 1.4 fusion.43
  134.0 1.4 fusion.43
  135.6 1.6 broadcast_in_dim.74
  138.1 28.5 %all_gather.26 = bf16[256,1024]{1,0:T(8,128)(2,1)} all-gather(bf16[256,128]{1,0:T(8,128)(2,1)S(1)} %copy-done.2), channel_id=1, replica_groups=mesh['dp'=8,'seq'=4] {'dp'}, dimensions={1}, use_global_device_ids=true | all-gather | bytes 589824 | tf_op jit(solution)/shard_map/all_gather | solution.py:103
  166.6 6.1 %all-gather = f32[2048,16]{0,1:T(8,128)S(1)} all-gather(f32[512,16]{0,1:T(8,128)S(1)} %get-tuple-element.146), channel_id=2, replica_groups=mesh['dp'=8,'seq'=4] {'seq'}, dimensions={0}, use_global_device_ids=true | all-gather | bytes 163840 | tf_op jit(solution)/shard_map/all_gather | solution.py:89
  172.8 6.2 %all-gather.1 = f32[2048,16]{0,1:T(8,128)S(1)} all-gather(f32[512,16]{0,1:T(8,128)S(1)} %get-tuple-element.147), channel_id=3, replica_groups=mesh['dp'=8,'seq'=4] {'seq'}, dimensions={0}, use_global_device_ids=true | all-gather | bytes 163840 | tf_op jit(solution)/shard_map/all_gather | solution.py:88
  179.1 17.9 %all-gather.14.cloned.1.call-done = f32[2048,1024]{0,1:T(8,128)} async-done(((f32[512,1024]{0,1:T(8,128)}), f32[2048,1024]{0,1:T(8,128)}) %all-gather.14.cloned.1.call-update) | async-done | bytes 8388624 | tf_op jit(solution)/shard_map/all_gather | solution.py:87
  197.1 10.9 %reshape.53 = f32[4,512,1024]{1,0,2:T(4,128)} reshape(f32[2048,1024]{0,1:T(8,128)} %all-gather.14.cloned.1.call-done) | data formatting | bytes 16777216 | tf_op jit(solution)/shard_map/all_gather | solution.py:87
  208.0 3.0 %fusion.16 = f32[128,1024]{0,1:T(8,128)S(1)} fusion(f32[4,512,1024]{1,0,2:T(4,128)} %reshape.53, s32[]{:T(128)S(6)} %select_n.45, f32[4,128,16]{1,0,2:T(4,128)S(1)} %get-tuple-element.179), kind=kLoop, calls=%fused_computation.21 | loop fusion | flops 917504 | bytes 2654212 | tf_op jit(solution)/shard_map/reduce_sum | solution.py:99
  211.1 10.1 %all-gather.12.cloned.1.call-done = bf16[1024,1024]{1,0:T(8,128)(2,1)} async-done(((bf16[256,1024]{1,0:T(8,128)(2,1)}), bf16[1024,1024]{1,0:T(8,128)(2,1)}) %all-gather.12.cloned.1.call-update) | async-done | bytes 2097168 | tf_op jit(solution)/shard_map/all_gather | solution.py:104
  221.1 2.1 fusion.30
  (138 shorter events, 48.3 us)
Async XLA Ops:
  6.5 51.5 %copy-start = (bf16[1,128,1024]{2,1,0:T(8,128)(2,1)S(1)}, bf16[1,128,1024]{2,1,0:T(8,128)(2,1)}, u32[]{:S(2)}) copy-start(bf16[1,128,1024]{2,1,0:T(8,128)(2,1)} %param.14) | copy-start | bytes 786436
  6.5 51.5 %copy-start.3 = (f32[3072]{0:T(1024)S(1)}, f32[3072]{0:T(1024)}, u32[]{:S(2)}) copy-start(f32[3072]{0:T(1024)} %param.18) | copy-start | bytes 36868
  6.5 51.5 %all-gather.8.cloned.1.call-start = ((), (), s32[]{:S(2)}) async-start(), calls=%async_computation | async-start | bytes 7864320 | tf_op jit(solution)/shard_map/all_gather | solution.py:37
  7.3 72.8 %all-gather.10.cloned.1.call-start = ((), (), s32[]{:S(2)}) async-start(), calls=%async_computation.1 | async-start | bytes 1310720 | tf_op jit(solution)/shard_map/all_gather | solution.py:44
  62.2 0.9 copy-start.7
  62.2 3.2 %copy-start.8 = (s32[8]{0:T(128)S(1)}, s32[8]{0:T(128)}, u32[]{:S(2)}) copy-start(s32[8]{0:T(128)} %param.24) | copy-start | bytes 100
  62.2 3.7 %copy-start.9 = (s32[8]{0:T(128)S(1)}, s32[8]{0:T(128)}, u32[]{:S(2)}) copy-start(s32[8]{0:T(128)} %param.23) | copy-start | bytes 100
  63.0 5.4 %copy-start.1 = (bf16[1,512,1024]{2,1,0:T(8,128)(2,1)S(1)}, bf16[1,512,1024]{2,1,0:T(8,128)(2,1)}, u32[]{:S(2)}) copy-start(bf16[1,512,1024]{2,1,0:T(8,128)(2,1)} %param.15) | copy-start | bytes 3145732
  63.0 134.1 %all-gather.14.cloned.1.call-start = ((), (), s32[]{:S(2)}) async-start(), calls=%async_computation.3 | async-start | bytes 10485760 | tf_op jit(solution)/shard_map/all_gather | solution.py:87
  137.2 0.8 copy-start.2
  137.2 83.9 %all-gather.12.cloned.1.call-start = ((), (), s32[]{:S(2)}) async-start(), calls=%async_computation.2 | async-start | bytes 2621440 | tf_op jit(solution)/shard_map/all_gather | solution.py:104
  208.0 13.2 %copy-start.4 = (f32[1024]{0:T(1024)S(1)}, f32[1024]{0:T(1024)}, u32[]{:S(2)}) copy-start(f32[1024]{0:T(1024)} %param.20) | copy-start | bytes 12292
  211.1 12.4 %copy-start.5 = (f32[1024]{0:T(1024)S(1)}, f32[1024]{0:T(1024)}, u32[]{:S(2)}) copy-start(f32[1024]{0:T(1024)} %param.22) | copy-start | bytes 12292
  211.1 12.4 %copy-start.6 = (f32[1024]{0:T(1024)S(1)}, f32[1024]{0:T(1024)}, u32[]{:S(2)}) copy-start(f32[1024]{0:T(1024)} %param.21) | copy-start | bytes 12292
Sparse Core Ops, SparseCore 0:
  8.9 49.0 all-gather.7
  63.1 16.8 all-gather.9
  137.4 59.6 all-gather.13
  198.5 22.5 all-gather.11
where the time goes:
time: 233 us; the launch traced here: 231 us
  waiting for transfers between devices  88.6 us (38%)
  matrix products  51.2 us (22%)
  blocking collectives  40.8 us (18%)
  local copies, waits for them, and re-layouts  17.2 us (7%)
  other arithmetic  17.2 us (7%)
  between operations  15 us (6%)
    all_gather x1, waiting for transfers between devices, local(): qkv_full = lax.all_gather(qkv_weight, 'seq', axis=1, tiled=True)  50.7 us
    all_gather x1, blocking collectives, local(): head_rows = lax.all_gather(out_weight, 'dp', axis=1, tiled=True)  28.5 us
    dot_general x16, matrix products, attend(): jnp.dot(weights.astype(jnp.bfloat16), value_block, preferred_element_type...  22.8 us
    dot_general x16, matrix products, attend(): lax.dot_general(query, key_block, (((1,), (1,)), ((), ())), preferred_ele...  22.5 us
    all_gather x1, waiting for transfers between devices, local(): lax.all_gather(partial_wide[None], 'seq', axis=0, tiled=True)  17.9 us
    all_gather x1, local copies, waits for them, and re-layouts, local(): lax.all_gather(partial_wide[None], 'seq', axis=0, tiled=True)  10.9 us
    all_gather x1, waiting for transfers between devices, local(): out_full = lax.all_gather(head_rows, 'seq', axis=0, tiled=True)  10.1 us
    all_gather x1, waiting for transfers between devices, local(): all_queries = lax.all_gather(own_queries, 'seq', axis=0, tiled=True)  9.1 us
  transfers between devices with their start and end apart: 4, of which 4 were waited for; matrix products, arithmetic and copies ran while one was open for 9% of the time, Pallas kernels for 0%

commit v1 on v0

--- a/solution.py
+++ b/solution.py
@@ -101,7 +101,12 @@
         .astype(jnp.bfloat16)
     )
     head_rows = lax.all_gather(out_weight, "dp", axis=1, tiled=True)
-    out_full = lax.all_gather(head_rows, "seq", axis=0, tiled=True)
+    ring = [head_rows]
+    for hop in range(3):
+        ring.append(lax.ppermute(ring[-1], "seq", [(dev, (dev + 1) % 4) for dev in range(4)]))
+    out_full = jnp.roll(
+        jnp.concatenate(ring[::-1], axis=0), (lax.axis_index("seq") + 1) * ring[0].shape[0], axis=0
+    )
     projected_out = jnp.dot(attn, out_full, preferred_element_type=jnp.float32)
     mixed = projected_out + out_bias + inputs.astype(jnp.float32)
     center = mixed - jnp.mean(mixed, axis=1, keepdims=True)

time: 233 us -> 251 us (1.077)
  waiting for transfers between devices: 88.6 us -> 109 us
  blocking collectives: 40.8 us -> 38 us
    ppermute x0 -> x3, waiting for transfers between devices: none -> 48.2 us  [local(): lax.ppermute(ring[-1], 'seq', [(dev, (dev + 1) % 4) for dev in range(4)])]
    all_gather x1, waiting for transfers between devices: 17.9 us -> 0.02 us  [local(): lax.all_gather(partial_wide[None], 'seq', axis=0, tiled=True)]
    all_gather x1 -> x0, waiting for transfers between devices: 10.1 us -> none  [local(): out_full = lax.all_gather(head_rows, 'seq', axis=0, tiled=True)]
  transfers between devices with their start and end apart: 4 -> 6, of which waited for: 4 -> 5; matrix products, arithmetic and copies ran while one was open for 9% -> 3% of each run, Pallas kernels for 0% -> 0%
where the time goes in v1:
time: 251 us; the launch traced here: 250 us
  waiting for transfers between devices  109 us (43%)
  matrix products  51.2 us (20%)
  blocking collectives  38 us (15%)
  local copies, waits for them, and re-layouts  18.6 us (7%)
  other arithmetic  17.3 us (7%)
  between operations  15.1 us (6%)
    all_gather x1, waiting for transfers between devices, local(): qkv_full = lax.all_gather(qkv_weight, 'seq', axis=1, tiled=True)  50.7 us
    ppermute x3, waiting for transfers between devices, local(): lax.ppermute(ring[-1], 'seq', [(dev, (dev + 1) % 4) for dev in range(4)])  48.2 us
    all_gather x1, blocking collectives, local(): head_rows = lax.all_gather(out_weight, 'dp', axis=1, tiled=True)  27.1 us
    dot_general x16, matrix products, attend(): jnp.dot(weights.astype(jnp.bfloat16), value_block, preferred_element_type...  22.8 us
    dot_general x16, matrix products, attend(): lax.dot_general(query, key_block, (((1,), (1,)), ((), ())), preferred_ele...  22.5 us
    all_gather x1, local copies, waits for them, and re-layouts, local(): lax.all_gather(partial_wide[None], 'seq', axis=0, tiled=True)  10.8 us
    all_gather x1, waiting for transfers between devices, local(): all_queries = lax.all_gather(own_queries, 'seq', axis=0, tiled=True)  9.1 us
    reduce_sum x16, other arithmetic, attend(): total = jnp.sum(weights, axis=1)  7.31 us
  transfers between devices with their start and end apart: 6, of which 5 were waited for; matrix products, arithmetic and copies ran while one was open for 3% of the time, Pallas kernels for 0%

profile of v1, /device:TPU:0, one launch (start us, length us, event | category | flops | bytes accessed | tf_op | source)
XLA Modules:
  0.0 249.8 jit_solution(15147377718544319950)
XLA Ops:
  7.3 50.7 %all-gather.7.cloned.1.call-done = bf16[1024,3072]{1,0:T(8,128)(2,1)} async-done(((bf16[1024,768]{1,0:T(8,128)(2,1)}), bf16[1024,3072]{1,0:T(8,128)(2,1)}) %all-gather.7.cloned.1.call-update) | async-done | bytes 6291472 | tf_op jit(solution)/shard_map/all_gather | solution.py:37
  58.0 3.8 %fusion.15 = bf16[128,3072]{1,0:T(8,128)(2,1)S(1)} fusion(bf16[1024,3072]{1,0:T(8,128)(2,1)} %all-gather.7.cloned.1.call-done, f32[3072]{0:T(1024)} %param.18, bf16[1,128,1024]{2,1,0:T(8,128)(2,1)} %param.14), kind=kOutput, calls=%fused_computation.19 | convolution fusion | flops 806092800 | bytes 7352320 | tf_op jit(solution)/shard_map/dot_general | solution.py:38
  68.4 2.6 %pad_maximum_fusion = (bf16[640,1024]{1,0:T(8,128)(2,1)S(1)}, bf16[640,1024]{1,0:T(8,128)(2,1)}) fusion(bf16[128,1024]{1,0:T(8,128)(2,1)S(1)} %copy.14, bf16[512,1024]{1,0:T(8,128)(2,1)S(1)} %bitcast.38, bf16[128,1024]{1,0:T(8,128)(2,1)S(1)} %copy.15, bf16[512,1024]{1,0:T(8,128)(2,1)} %bitcast.39), kind=kLoop, calls=%fused_computation.24 | loop fusion | flops 5242880 | bytes 5242880 | tf_op jit(solution)/shard_map/concatenate | solution.py:45
  71.0 9.1 %all-gather.9.cloned.1.call-done = bf16[512,1024]{0,1:T(8,128)(2,1)} async-done(((bf16[128,1024]{0,1:T(8,128)(2,1)}), bf16[512,1024]{0,1:T(8,128)(2,1)}) %all-gather.9.cloned.1.call-update) | async-done | bytes 1048592 | tf_op jit(solution)/shard_map/all_gather | solution.py:44
  80.1 55.4 %while.17 = (s32[]{:T(128)}, bf16[512,1024]{0,1:T(8,128)(2,1)S(1)}, f32[512,16]{0,1:T(8,128)S(1)}, f32[512,16]{0,1:T(8,128)S(1)}, bf16[512,1024]{0,1:T(8,128)(2,...) while((s32[]{:T(128)}, bf16[512,1024]{0,1:T(8,128)(2,1)S(1)}, ...), condition=%wide.region_3.4_spmd, body=%wide.region_0.3_spmd.sunk | while | flops 86900224 | bytes 5398699 | solution.py:84
  82.0 1.4 fusion.50
  89.0 1.4 fusion.50
  95.9 1.4 fusion.50
  102.8 1.4 fusion.50
  106.3 1.4 fusion.50
  113.2 1.4 fusion.50
  120.1 1.4 fusion.50
  127.1 1.4 fusion.50
  135.6 1.6 broadcast_in_dim.74
  137.3 27.1 %all_gather.23 = bf16[256,1024]{1,0:T(8,128)(2,1)S(1)} all-gather(bf16[256,128]{1,0:T(8,128)(2,1)S(1)} %copy-done.3), channel_id=1, replica_groups=mesh['dp'=8,'seq'=4] {'dp'}, dimensions={1}, use_global_device_ids=true | all-gather | bytes 589824 | tf_op jit(solution)/shard_map/all_gather | solution.py:103
  164.4 19.8 %collective-permute-done = bf16[256,1024]{1,0:T(8,128)(2,1)S(1)} collective-permute-done((bf16[256,1024]{1,0:T(8,128)(2,1)S(1)}, bf16[256,1024]{1,0:T(8,128)(2,1)S(1)}, u32[]{:S(2)}, u32[]{:S(2)}) %collective-permute-start) | collective-permute-done | bytes 524320 | tf_op jit(solution)/shard_map/ppermute | solution.py:106
  184.2 19.8 %collective-permute-done.1 = bf16[256,1024]{1,0:T(8,128)(2,1)S(1)} collective-permute-done((bf16[256,1024]{1,0:T(8,128)(2,1)S(1)}, bf16[256,1024]{1,0:T(8,128)(2,1)S(1)}, u32[]{:S(2)}, u32[]{:S(2)}) %collective-permute-start.1) | collective-permute-done | bytes 524320 | tf_op jit(solution)/shard_map/ppermute | solution.py:106
  204.0 8.6 %collective-permute-done.2 = bf16[256,1024]{1,0:T(8,128)(2,1)S(1)} collective-permute-done((bf16[256,1024]{1,0:T(8,128)(2,1)S(1)}, bf16[256,1024]{1,0:T(8,128)(2,1)S(1)}, u32[]{:S(2)}, u32[]{:S(2)}) %collective-permute-start.2) | collective-permute-done | bytes 524320 | tf_op jit(solution)/shard_map/ppermute | solution.py:106
  213.0 1.9 copy-done.1
  214.9 5.4 %all-gather = f32[2048,16]{0,1:T(8,128)S(1)} all-gather(f32[512,16]{0,1:T(8,128)S(1)} %get-tuple-element.146), channel_id=2, replica_groups=mesh['dp'=8,'seq'=4] {'seq'}, dimensions={0}, use_global_device_ids=true | all-gather | bytes 163840 | tf_op jit(solution)/shard_map/all_gather | solution.py:89
  220.4 5.4 %all-gather.1 = f32[2048,16]{0,1:T(8,128)S(1)} all-gather(f32[512,16]{0,1:T(8,128)S(1)} %get-tuple-element.147), channel_id=3, replica_groups=mesh['dp'=8,'seq'=4] {'seq'}, dimensions={0}, use_global_device_ids=true | all-gather | bytes 163840 | tf_op jit(solution)/shard_map/all_gather | solution.py:88
  226.0 10.8 %reshape.53 = f32[4,512,1024]{1,0,2:T(4,128)} reshape(f32[2048,1024]{0,1:T(8,128)} %all-gather.11.cloned.1.call-done) | data formatting | bytes 16777216 | tf_op jit(solution)/shard_map/all_gather | solution.py:87
  236.8 3.1 %fusion.16 = f32[128,1024]{0,1:T(8,128)S(1)} fusion(f32[4,512,1024]{1,0,2:T(4,128)} %reshape.53, s32[]{:T(128)S(6)} %select_n.58, f32[4,128,16]{1,0,2:T(4,128)S(1)} %get-tuple-element.179), kind=kLoop, calls=%fused_computation.21 | loop fusion | flops 917504 | bytes 2654212 | tf_op jit(solution)/shard_map/reduce_sum | solution.py:99
  240.0 2.1 fusion.38
  (149 shorter events, 50.6 us)
Async XLA Ops:
  6.5 51.5 %all-gather.7.cloned.1.call-start = ((), (), s32[]{:S(2)}) async-start(), calls=%async_computation | async-start | bytes 7864320 | tf_op jit(solution)/shard_map/all_gather | solution.py:37
  7.3 72.8 %all-gather.9.cloned.1.call-start = ((), (), s32[]{:S(2)}) async-start(), calls=%async_computation.1 | async-start | bytes 1310720 | tf_op jit(solution)/shard_map/all_gather | solution.py:44
  61.8 1.3 copy-start.7
  61.8 3.6 %copy-start.8 = (s32[8]{0:T(128)S(1)}, s32[8]{0:T(128)}, u32[]{:S(2)}) copy-start(s32[8]{0:T(128)} %param.24) | copy-start | bytes 100
  61.8 4.1 %copy-start.9 = (s32[8]{0:T(128)S(1)}, s32[8]{0:T(128)}, u32[]{:S(2)}) copy-start(s32[8]{0:T(128)} %param.23) | copy-start | bytes 100
  62.2 6.2 %copy-start.2 = (bf16[1,512,1024]{2,1,0:T(8,128)(2,1)S(1)}, bf16[1,512,1024]{2,1,0:T(8,128)(2,1)}, u32[]{:S(2)}) copy-start(bf16[1,512,1024]{2,1,0:T(8,128)(2,1)} %param.15) | copy-start | bytes 3145732
  63.0 163.0 %all-gather.11.cloned.1.call-start = ((), (), s32[]{:S(2)}) async-start(), calls=%async_computation.2 | async-start | bytes 10485760 | tf_op jit(solution)/shard_map/all_gather | solution.py:87
  135.6 1.7 copy-start.3
  164.4 19.8 %collective-permute-start = (bf16[256,1024]{1,0:T(8,128)(2,1)S(1)}, bf16[256,1024]{1,0:T(8,128)(2,1)S(1)}, u32[]{:S(2)}, u32[]{:S(2)}) collective-permute-start(bf16[256,1024]{1,0:T(8,128)(2,1)S(1)} %all_gather.23), channel_id=1, source_target_pairs={{0,1},{1,2},{2,3},{3,0},{4,5},{5,6},{6,7},{7,4},{8,9},{9,10},{10,1... | collective-permute-start | bytes 1572872 | tf_op jit(solution)/shard_map/ppermute | solution.py:106
  184.2 19.8 %collective-permute-start.1 = (bf16[256,1024]{1,0:T(8,128)(2,1)S(1)}, bf16[256,1024]{1,0:T(8,128)(2,1)S(1)}, u32[]{:S(2)}, u32[]{:S(2)}) collective-permute-start(bf16[256,1024]{1,0:T(8,128)(2,1)S(1)} %collective-permute-done), channel_id=1, source_target_pairs={{0,1},{1,2},{2,3},{3,0},{4,5},{5,6},{6,7},{7,4},{8,9},{9,10},{10,1... | collective-permute-start | bytes 1572872 | tf_op jit(solution)/shard_map/ppermute | solution.py:106
  204.0 8.6 %collective-permute-start.2 = (bf16[256,1024]{1,0:T(8,128)(2,1)S(1)}, bf16[256,1024]{1,0:T(8,128)(2,1)S(1)}, u32[]{:S(2)}, u32[]{:S(2)}) collective-permute-start(bf16[256,1024]{1,0:T(8,128)(2,1)S(1)} %collective-permute-done.1), channel_id=1, source_target_pairs={{0,1},{1,2},{2,3},{3,0},{4,5},{5,6},{6,7},{7,4},{8,9},{9,10},{10,1... | collective-permute-start | bytes 1572872 | tf_op jit(solution)/shard_map/ppermute | solution.py:106
  213.0 1.9 copy-start.1
  236.8 3.1 %copy-start = (bf16[1,128,1024]{2,1,0:T(8,128)(2,1)S(1)}, bf16[1,128,1024]{2,1,0:T(8,128)(2,1)}, u32[]{:S(2)}) copy-start(bf16[1,128,1024]{2,1,0:T(8,128)(2,1)} %param.14) | copy-start | bytes 786436
  236.8 3.2 %copy-start.4 = (f32[1024]{0:T(1024)S(1)}, f32[1024]{0:T(1024)}, u32[]{:S(2)}) copy-start(f32[1024]{0:T(1024)} %param.20) | copy-start | bytes 12292
  239.9 2.5 copy-start.5
  239.9 2.5 copy-start.6
Sparse Core Ops, SparseCore 0:
  8.9 49.0 all-gather.6
  63.1 16.8 all-gather.8
  137.4 69.5 all-gather.10
